TPU v7x, 256 devices: a whole 4x4x8 slice. The times are simulated.
256 devices in a mesh: ctx: 8 (over x, z_hi), chan: 8 (over z_lo, core), rep: 4 (over y).
Axes of the slice: x: 4, y: 4, z: 8 (z_hi: 2, z_lo: 4; z = z_hi * 4 + z_lo), core: 2. Of those that a mesh axis runs over, the one named last changes fastest.
Arguments:
- values_in: bfloat16 [4, 2048, 4096], P('rep', 'ctx', 'chan'), may hold values from -6 to 6
- keys_in: bfloat16 [4, 2048, 4096], P('rep', 'ctx', 'chan'), may hold values from -6 to 6
- query_in: bfloat16 [4, 2048, 4096], P('rep', 'ctx', 'chan'), may hold values from -6 to 6
- cotangent: bfloat16 [4, 2048, 4096], P('rep', 'ctx', 'chan'), may hold values from -6 to 6
- out_weight: bfloat16 [4096, 4096], P(None, 'chan'), may hold values from -0.09375 to 0.09375
- residues: float32 [16, 256], P(None, 'chan'), may hold values from -0.2581989 to 0.2581989
- rates: float32 [16, 256], P(None, 'chan'), may hold values from 9.765625e-05 to 0.0333333333
Outputs:
- output: bfloat16 [4, 2048, 4096], P('rep', 'ctx', 'chan')
- grad_values: bfloat16 [4, 2048, 4096], P('rep', 'ctx', 'chan')
- grad_keys: bfloat16 [4, 2048, 4096], P('rep', 'ctx', 'chan')
- grad_query: bfloat16 [4, 2048, 4096], P('rep', 'ctx', 'chan')
- grad_residues: float32 [16, 256], P(None, 'chan')
- grad_rates: float32 [16, 256], P(None, 'chan')
All inputs are finite; a program needn't handle non-finite values.
Results may differ from a plain program's by a relative error of at most 0.013.
Values may be sent and summed in bfloat16 or wider, within the bound.
A program may use at most 128 MiB of HBM per device.

v0:
```python
import jax
import jax.numpy as jnp
from jax import lax
from jax.sharding import PartitionSpec as P

GROUP = 16


def entering(value, axis, join, neutral, backward):
    count, mine = (lax.axis_size(axis), lax.axis_index(axis))
    pieces = jax.tree.map(lambda part: lax.all_gather(part, axis), value)
    if backward:
        pieces = jax.tree.map(lambda part: part[::-1], pieces)
        mine = count - 1 - mine
    running = jax.tree.map(
        lambda part, zero: jnp.full_like(part, 0) + jnp.asarray(zero, part.dtype), value, neutral
    )

    def step(position, running):
        longer = join(running, jax.tree.map(lambda part: part[position], pieces))
        return jax.tree.map(lambda new, old: jnp.where(position < mine, new, old), longer, running)

    return lax.fori_loop(0, count - 1, step, running)


def combine_states(earlier, later):
    early_a, early_len, early_s, early_p = earlier
    late_a, late_len, late_s, late_p = later
    return (
        early_a * late_a,
        early_len + late_len,
        late_a * early_s + late_s,
        late_a * (early_p + late_len * early_s) + late_p,
    )


def combine_suffix(earlier, later):
    early_a, early_q = earlier
    late_a, late_q = later
    return (early_a * late_a, late_a * early_q + late_q)


def toeplitz_upper(filter_taps):
    block_len, groups = filter_taps.shape
    padded = jnp.concatenate([filter_taps, jnp.zeros_like(filter_taps)], axis=0)
    stream = jnp.tile(padded, (block_len, 1))
    return stream[: block_len * (2 * block_len - 1)].reshape(block_len, 2 * block_len - 1, groups)[
        :, :block_len
    ]


def shear_sum(mixed):
    groups, block_len, _ = mixed.shape
    padded = jnp.pad(mixed, ((0, 0), (0, 0), (0, block_len)))
    flat = padded.reshape(groups, 2 * block_len * block_len)
    flat = jnp.pad(flat, ((0, 0), (0, block_len)))
    shifted = flat.reshape(groups, block_len, 2 * block_len + 1)[:, :, :block_len]
    return jnp.sum(shifted, axis=1).T


def per_device(values_in, keys_in, query_in, cotangent, out_weight, residues, rates):
    highest = lax.Precision.HIGHEST
    tokens = values_in.shape[1]
    channels = values_in.shape[2]
    pole_count = residues.shape[0]
    groups = channels // GROUP
    block_len = min(128, tokens // 2)
    blocks = tokens // block_len
    k_float = keys_in[0].astype(jnp.float32)
    v_float = values_in[0].astype(jnp.float32)
    q_float = query_in[0].astype(jnp.float32)
    z_round = lax.optimization_barrier((k_float * v_float).astype(jnp.bfloat16))
    z_blocks = z_round.astype(jnp.float32).reshape(blocks, block_len, groups, GROUP)
    lag_pos = jnp.arange(block_len, dtype=jnp.float32)
    decay_table = jnp.exp(-lag_pos[:, None, None] * rates[None])
    end_decay = jnp.exp(-(block_len - lag_pos)[:, None, None] * rates[None])
    block_decay = jnp.exp(-block_len * rates)[:, :, None]
    filter_taps = jnp.einsum("lrg,rg->lg", decay_table, residues, precision=highest)
    toeplitz = toeplitz_upper(filter_taps)
    local_conv = jnp.einsum("stg,bsgk->btgk", toeplitz, z_blocks, precision=highest)
    state_z = jnp.einsum("jrg,bjgk->brgk", end_decay, z_blocks, precision=highest)
    state_p = jnp.einsum(
        "jrg,bjgk->brgk",
        end_decay * (block_len - lag_pos)[:, None, None],
        z_blocks,
        precision=highest,
    )

    def forward_block(carry, item):
        s_now, p_now = carry
        z_item, p_item = item
        return (
            (block_decay * s_now + z_item, block_decay * (p_now + block_len * s_now) + p_item),
            carry,
        )

    zero_state = jnp.zeros((pole_count, groups, GROUP), jnp.float32)
    (slab_s, slab_p), (pre_s, pre_p) = lax.scan(
        forward_block, (zero_state, zero_state), (state_z, state_p)
    )
    slab_decay = jnp.broadcast_to(
        jnp.exp(-tokens * rates)[:, :, None], (pole_count, groups, GROUP)
    ).reshape(pole_count, channels)
    zeros_flat = jnp.zeros((pole_count, channels), jnp.float32)
    ones_flat = jnp.ones((pole_count, channels), jnp.float32)
    slab_length = jnp.full((pole_count, channels), float(tokens), jnp.float32)
    mine = (
        slab_decay,
        slab_length,
        slab_s.reshape(pole_count, channels),
        slab_p.reshape(pole_count, channels),
    )
    prefix = entering(
        mine, "ctx", combine_states, (ones_flat, zeros_flat, zeros_flat, zeros_flat), False
    )
    in_s = prefix[2]
    in_p = prefix[3]
    in_s3 = in_s.reshape(pole_count, groups, GROUP)
    in_p3 = in_p.reshape(pole_count, groups, GROUP)
    offsets = jnp.arange(blocks, dtype=jnp.float32) * block_len
    power = jnp.exp(-offsets[:, None, None] * rates[None])[..., None]
    block_s = power * in_s3[None] + pre_s
    block_p = power * (in_p3[None] + offsets[:, None, None, None] * in_s3[None]) + pre_p
    carried = jnp.einsum("irg,brgk->bigk", decay_table * residues[None], block_s, precision=highest)
    conv = (local_conv + carried).reshape(tokens, channels)
    gated = (q_float * conv).astype(jnp.bfloat16)
    contract_last = (((1,), (1,)), ((), ()))
    turned_once = lax.all_to_all(out_weight, "chan", split_axis=0, concat_axis=1, tiled=True)
    output = lax.dot_general(
        lax.all_gather(gated, "chan", axis=1, tiled=True),
        turned_once,
        contract_last,
        preferred_element_type=jnp.float32,
    ).astype(jnp.bfloat16)
    back = jnp.dot(
        lax.all_gather(cotangent[0], "chan", axis=1, tiled=True),
        out_weight,
        preferred_element_type=jnp.float32,
    )
    dconv = q_float * back
    grad_query = (conv * back).astype(jnp.bfloat16)
    dconv_blocks = dconv.reshape(blocks, block_len, groups, GROUP)
    grad_lag = jnp.einsum("irg,bigk->brgk", decay_table, dconv_blocks, precision=highest)
    grad_pos = jnp.einsum(
        "irg,bigk->brgk", decay_table * lag_pos[:, None, None], dconv_blocks, precision=highest
    )

    def backward_block(q_now, d_item):
        return (block_decay * q_now + d_item, q_now)

    slab_q, post_q = lax.scan(backward_block, zero_state, grad_lag, reverse=True)
    mine_back = (slab_decay, slab_q.reshape(pole_count, channels))
    suffix = entering(mine_back, "ctx", combine_suffix, (ones_flat, zeros_flat), True)
    in_q = suffix[1]
    in_q3 = in_q.reshape(pole_count, groups, GROUP)
    remain = (blocks - 1) * block_len - offsets
    after = jnp.exp(-remain[:, None, None] * rates[None])[..., None]
    block_q = after * in_q3[None] + post_q
    dz_local = jnp.einsum("stg,btgk->bsgk", toeplitz, dconv_blocks, precision=highest)
    dz_carried = jnp.einsum(
        "jrg,brgk->bjgk", end_decay * residues[None], block_q, precision=highest
    )
    dz_field = (dz_local + dz_carried).reshape(tokens, channels)
    grad_values = (dz_field * k_float).astype(jnp.bfloat16)
    grad_keys = (dz_field * v_float).astype(jnp.bfloat16)
    mixed = jnp.einsum("bsgk,btgk->gst", z_blocks, dconv_blocks, precision=highest)
    lag_sums = shear_sum(mixed)
    res_local = jnp.einsum("lg,lrg->rg", lag_sums, decay_table, precision=highest) + jnp.sum(
        grad_lag * block_s, axis=(0, 3)
    )
    rate_inner = jnp.einsum(
        "lg,lrg->rg", lag_sums * lag_pos[:, None], decay_table, precision=highest
    )
    rate_local = -residues * (
        rate_inner + jnp.sum(grad_pos * block_s + grad_lag * block_p, axis=(0, 3))
    )
    grad_residues, grad_rates = lax.psum((res_local, rate_local), ("ctx", "rep"))
    return (
        output[None],
        grad_values[None],
        grad_keys[None],
        grad_query[None],
        grad_residues,
        grad_rates,
    )


def solution(mesh):
    return jax.shard_map(
        per_device,
        mesh=mesh,
        in_specs=(
            P("rep", "ctx", "chan"),
            P("rep", "ctx", "chan"),
            P("rep", "ctx", "chan"),
            P("rep", "ctx", "chan"),
            P(None, "chan"),
            P(None, "chan"),
            P(None, "chan"),
        ),
        out_specs=(
            P("rep", "ctx", "chan"),
            P("rep", "ctx", "chan"),
            P("rep", "ctx", "chan"),
            P("rep", "ctx", "chan"),
            P(None, "chan"),
            P(None, "chan"),
        ),
        check_vma=False,
    )
```

profile of v0, /device:TPU:96, one launch (start us, length us, event | category | flops | bytes accessed | tf_op | source)
XLA Modules:
  0.0 586.6 jit_solution(13105508236607143715)
XLA Ops:
  7.9 5.5 all-to-all-start
  17.0 132.8 %all_gather.21 = f32[8,16,512]{2,1,0:T(8,128)S(1)} all-gather(f32[1,16,512]{2,1,0:T(8,128)S(1)} %all_gather_reshape.14), channel_id=1, replica_groups=mesh['ctx'=8,'chan'=8,'rep'=4] {'ctx'}, dimensions={0}, use_global_device_ids=true | all-gather | bytes 294912 | tf_op jit(solution)/shard_map/all_gather | solution.py:11
  149.7 44.4 %all_gather.22 = f32[8,16,512]{2,1,0:T(8,128)S(1)} all-gather(f32[1,16,512]{2,1,0:T(8,128)S(1)} %all_gather_reshape.15), channel_id=1, replica_groups=mesh['ctx'=8,'chan'=8,'rep'=4] {'ctx'}, dimensions={0}, use_global_device_ids=true | all-gather | bytes 294912 | tf_op jit(solution)/shard_map/all_gather | solution.py:11
  194.2 44.3 %all_gather.20 = f32[8,16,512]{2,1,0:T(8,128)S(1)} all-gather(f32[1,16,512]{2,1,0:T(8,128)S(1)} %all_gather_reshape.13), channel_id=1, replica_groups=mesh['ctx'=8,'chan'=8,'rep'=4] {'ctx'}, dimensions={0}, use_global_device_ids=true | all-gather | bytes 294912 | tf_op jit(solution)/shard_map/all_gather | solution.py:11
  241.3 2.4 copy.193
  243.7 2.2 slice.12
  246.0 9.4 %reshape.87 = f32[128,255,32]{1,0,2:T(8,128)} reshape(f32[32640,32]{0,1:T(8,128)} %slice.12) | data formatting | bytes 8355840 | tf_op jit(solution)/shard_map/reshape | solution.py:47
  256.1 2.7 fusion.8
  260.7 5.1 fusion.24
  265.8 2.0 copy.158
  267.8 1.3 reshape.89
  269.1 1.0 convolution_bitcast_fusion
  270.7 2.4 copy.195
  273.1 2.3 pad.10
  275.4 8.0 %reshape.92 = f32[32,128,257]{2,1,0:T(8,128)} reshape(f32[32,32896]{1,0:T(8,128)} %pad.10) | data formatting | bytes 8421376 | tf_op jit(solution)/shard_map/reshape | solution.py:57
  284.5 1.7 slice_reduce_fusion
  286.9 1.8 fusion.13
  289.3 217.7 %all-reduce.3 = (f32[16,32]{0,1:T(8,128)S(1)}, f32[16,32]{0,1:T(8,128)S(1)}) all-reduce(f32[16,32]{0,1:T(8,128)S(1)} %add.167, f32[16,32]{0,1:T(8,128)S(1)} %add_multiply_fusion), channel_id=1, replica_groups=mesh['ctx'=8,'chan'=8,'rep'=4] {'ctx','rep'}, use_global_device_ids=true, to_apply=%region_10.11 | all-reduce | flops 1024 | bytes 8192 | tf_op jit(solution)/shard_map/psum | solution.py:177
  508.9 45.0 %all_gather.25 = f32[8,16,512]{2,1,0:T(8,128)S(1)} all-gather(f32[1,16,512]{2,1,0:T(8,128)S(1)} %all_gather_reshape.16), channel_id=1, replica_groups=mesh['ctx'=8,'chan'=8,'rep'=4] {'ctx'}, dimensions={0}, use_global_device_ids=true | all-gather | bytes 294912 | tf_op jit(solution)/shard_map/all_gather | solution.py:11
  554.0 5.6 while.67
  561.0 4.9 fusion.10
  566.8 0.8 copy.173
  568.5 6.5 %copy.157 = bf16[512,8,512]{0,2,1:T(8,128)(2,1)} copy(bf16[512,8,512]{2,0,1:T(8,128)(2,1)} %bitcast.20) | data formatting | bytes 8388608 | tf_op jit(solution)/shard_map/all_to_all | solution.py:128
  575.0 4.8 fusion.14
  (111 shorter events, 23.1 us)
Async XLA Ops:
  7.2 253.5 %all-gather.6.cloned.1.call-start = ((), (), s32[]{:S(2)}) async-start(), calls=%async_computation.2 | async-start | bytes 2359296 | tf_op jit(solution)/shard_map/all_gather | solution.py:136
  7.9 5.6 copy-start.4
  7.9 5.7 copy-start.2
  7.9 5.8 copy-start.3
  7.9 560.5 %all-to-all-start = ((bf16[8,512,512]{2,1,0:T(8,128)(2,1)}), bf16[8,512,512]{2,1,0:T(8,128)(2,1)}, u32[]{:S(2)}, u32[]{:S(2)}) async-start(bf16[8,512,512]{2,1,0:T(8,128)(2,1)} %bitcast.196), calls=%async_computation | async-start | bytes 8388608 | tf_op jit(solution)/shard_map/all_to_all | solution.py:128
  13.4 561.5 %all-gather.4.cloned.1.call-start = ((), (), s32[]{:S(2)}) async-start(), calls=%async_computation.1 | async-start | bytes 2359296 | tf_op jit(solution)/shard_map/all_gather | solution.py:130
  16.0 223.6 %copy-start = (f32[2,16,32,16]{2,3,1,0:T(8,128)}, f32[2,16,32,16]{2,3,1,0:T(8,128)S(1)}, u32[]{:S(2)}) copy-start(f32[2,16,32,16]{2,3,1,0:T(8,128)S(1)} %get-tuple-element.393) | copy-start | bytes 196612
  16.1 224.3 %copy-start.5 = (f32[16,32]{1,0:T(8,128)S(1)}, f32[16,32]{1,0:T(8,128)}, u32[]{:S(2)}) copy-start(f32[16,32]{1,0:T(8,128)} %param.20) | copy-start | bytes 6148
  255.4 4.7 copy-start.1
Sparse Core Ops, SparseCore 0:
  9.8 76.7 all-gather.5
  508.5 31.4 all-gather.3
where the time goes:
time: 588 us; the launch traced here: 587 us
  blocking collectives  484 us (82%)
  local copies, waits for them, and re-layouts  48.1 us (8%)
  matrix products  24.9 us (4%)
  between operations  14.6 us (2%)
  other arithmetic  8.06 us (1%)
    all_gather x4, blocking collectives, entering(): pieces = jax.tree.map(lambda part: lax.all_gather(part, axis), value)  267 us
    psum x1, blocking collectives, per_device(): lax.psum((res_local, rate_local), ('ctx', 'rep'))  218 us
  transfers between devices with their start and end apart: 3, of which 0 were waited for; matrix products, arithmetic and copies ran while one was open for 13% of the time, Pallas kernels for 0%

commit v1 on v0

v1 whole, which is shorter than its diff:
```python
import functools

import jax
import jax.numpy as jnp
from jax import lax
from jax.experimental import pallas as pl
from jax.experimental.pallas import tpu as pltpu
from jax.sharding import PartitionSpec as P

GROUP = 16
F32 = jnp.float32
BF16 = jnp.bfloat16
MESH = pl.DeviceIdType.MESH


def iota(shape, axis):
    return lax.broadcasted_iota(jnp.int32, shape, axis)


def dot(a, b, ca=1, cb=0):
    return lax.dot_general(a, b, (((ca,), (cb,)), ((), ())), preferred_element_type=F32)


def dot_exact(a, b, ca=1, cb=0):
    return lax.dot_general(
        a, b, (((ca,), (cb,)), ((), ())), precision=lax.Precision.HIGHEST, preferred_element_type=F32
    )


def split(a):
    high = a.astype(BF16)
    return high, (a - high.astype(F32)).astype(BF16)


def kernel(
    v_ref, k_ref, q_ref, d_ref, w_hbm, rates_ref, res_ref,
    out_ref, gv_ref, gk_ref, gq_ref, gres_ref, grate_ref,
    w_ref, w_sem, own_sem,
    rate_col, res_col, rate_row, res_row, rate_chan,
    tab_u, tab_v, e_s, e_p, e_q, e_q1, row_f, row_b, row_v, row_u,
    z_ref, conv_ref, gated_ref, dconv_ref, back_ref, dz_ref,
    state_s, state_p, pair_s, pair_p, zin_s, zin_p, xin_s, xin_p, in_s, in_p,
    state_q, state_q1, pair_q, zin_q, xin_q, in_q,
    g_own, g_par, pacc, pbuf, xbuf, snd_r, snd_l, rec_l, rec_r,
    gsum, gout, gin_y, gin_x, gin_z,
    ag_send, ag_recv, agp_send, agp_recv,
    fz_send, fz_recv, fx_send, fx_recv, bx_send, bx_recv,
    p_send, p_recv, rr_send, rr_recv, rl_send, rl_recv, gs_send, gs_recv,
):
    chan = lax.axis_index("chan")
    ctx = lax.axis_index("ctx")
    rep = lax.axis_index("rep")
    core, zl = lax.rem(chan, 2), lax.div(chan, 2)
    zh, xx = lax.rem(ctx, 2), lax.div(ctx, 2)
    has_left, has_right = zl > 0, zl < 3
    left, right, partner = {"chan": chan - 2}, {"chan": chan + 2}, {"chan": chan + 1 - 2 * core}
    zpeer = {"ctx": ctx + 1 - 2 * zh}
    xpeer = [{"ctx": lax.rem(xx + i, 4) * 2 + zh} for i in (1, 2, 3)]
    ypeer = [{"rep": lax.rem(rep + i, 4)} for i in (1, 2, 3)]

    def remote(src, dst, ssem, rsem, dev):
        return pltpu.make_async_remote_copy(
            src_ref=src, dst_ref=dst, send_sem=ssem, recv_sem=rsem, device_id=dev, device_id_type=MESH
        )

    w_copy = pltpu.make_async_copy(w_hbm, w_ref, w_sem)
    w_copy.start()
    own_copy = pltpu.make_async_copy(d_ref, g_own.at[zl], own_sem)
    own_copy.start()
    barrier = pltpu.get_barrier_semaphore()
    for dev in [partner, zpeer] + xpeer + ypeer:
        pl.semaphore_signal(barrier, inc=1, device_id=dev, device_id_type=MESH)

    @pl.when(has_left)
    def _():
        pl.semaphore_signal(barrier, inc=1, device_id=left, device_id_type=MESH)

    @pl.when(has_right)
    def _():
        pl.semaphore_signal(barrier, inc=1, device_id=right, device_id_type=MESH)

    sel_col = jnp.where(lax.div(iota((512, 32), 0), 16) == iota((512, 32), 1), 1.0, 0.0).astype(F32)
    own_col = lax.rem(iota((512, 16), 0), 16) == iota((512, 16), 1)
    sel_row = jnp.where(lax.div(iota((32, 512), 1), 16) == iota((32, 512), 0), 1.0, 0.0).astype(F32)
    own_row = lax.rem(iota((16, 512), 1), 16) == iota((16, 512), 0)
    for src, col, row in ((rates_ref, rate_col, rate_row), (res_ref, res_col, res_row)):
        wide = dot_exact(sel_col, src[...], 1, 1)
        col[...] = jnp.sum(jnp.where(own_col, wide, 0.0), axis=1, keepdims=True)
        flat = dot_exact(src[...], sel_row)
        row[...] = jnp.sum(jnp.where(own_row, flat, 0.0), axis=0, keepdims=True)
        if src is rates_ref:
            rate_chan[...] = flat

    lane256 = iota((64, 256), 1).astype(F32)

    @pl.loop(0, 8)
    def _(i):
        rows = pl.ds(pl.multiple_of(i * 64, 64), 64)
        rate = rate_col[rows, :]
        left_over = 256.0 - lane256
        decay = jnp.exp(-rate * left_over)
        high, low = split(decay)
        e_s[0, rows, :] = high
        e_s[1, rows, :] = low
        e_p[rows, :] = (decay * left_over).astype(BF16)

    z_ref[...] = (k_ref[...].astype(F32) * v_ref[...].astype(F32)).astype(BF16)
    own_block = lax.div(iota((256, 256), 0), 16) == lax.div(iota((256, 256), 1), 16)

    def fold(a):
        return jnp.sum(jnp.where(own_block, a, 0.0).reshape(16, 16, 256), axis=0)

    def spread(s):
        return jnp.where(own_block, jnp.broadcast_to(s[None], (16, 16, 256)).reshape(256, 256), 0.0)

    for tile in range(2):
        part = slice(tile * 256, tile * 256 + 256)
        zt = z_ref[:, part]
        state_s[:, part] = fold(dot(e_s[0, part, :], zt) + dot(e_s[1, part, :], zt))
        state_p[:, part] = fold(dot(e_p[part, :], zt))

    pl.semaphore_wait(barrier, 8 + jnp.where(has_left, 1, 0) + jnp.where(has_right, 1, 0))

    fz = [
        remote(state_s, zin_s, fz_send.at[0], fz_recv.at[0], zpeer),
        remote(state_p, zin_p, fz_send.at[1], fz_recv.at[1], zpeer),
    ]
    for c in fz:
        c.start()

    def ag_right(src_ref, src, m):
        return remote(src_ref, g_own.at[src], ag_send.at[0, m], ag_recv.at[src], right)

    def ag_left(src_ref, src, m):
        return remote(src_ref, g_own.at[src], ag_send.at[1, m], ag_recv.at[src], left)

    def ag_partner(src_ref, src):
        return remote(src_ref, g_par.at[src], agp_send.at[src], agp_recv.at[src], partner)

    @pl.when(has_right)
    def _():
        ag_right(d_ref, zl, 0).start()

    @pl.when(has_left)
    def _():
        ag_left(d_ref, zl, 0).start()

    ag_partner(d_ref, zl).start()

    def ag_step(m):
        src_l, src_r = zl - m, zl + m

        @pl.when(src_l >= 0)
        def _():
            ag_right(g_own.at[src_l], src_l, 0).wait_recv()

            if m < 3:
                @pl.when(has_right)
                def _():
                    ag_right(g_own.at[src_l], src_l, m).start()

            ag_partner(g_own.at[src_l], src_l).start()

        @pl.when(src_r <= 3)
        def _():
            ag_left(g_own.at[src_r], src_r, 0).wait_recv()

            if m < 3:
                @pl.when(has_left)
                def _():
                    ag_left(g_own.at[src_r], src_r, m).start()

            ag_partner(g_own.at[src_r], src_r).start()

    def ag_drain():
        for m in range(3):
            @pl.when(jnp.logical_and(has_right, zl - m >= 0))
            def _():
                ag_right(d_ref, zl, m).wait_send()

            @pl.when(jnp.logical_and(has_left, zl + m <= 3))
            def _():
                ag_left(d_ref, zl, m).wait_send()

        for j in range(4):
            ag_partner(d_ref, j).wait_send()

    @pl.loop(0, 8)
    def _(i):
        rows = pl.ds(pl.multiple_of(i * 64, 64), 64)
        groups = pl.ds(i * 4, 4)
        rate, res = rate_col[rows, :], res_col[rows, :]
        centre = lane256 - 128.0
        u_high, u_low = split(res * jnp.exp(-rate * centre))
        v_high, v_low = split(jnp.exp(rate * centre))
        for at, uu, vv in ((0, u_high, v_high), (16, u_high, v_low), (32, u_low, v_high)):
            tab_u[groups, at : at + 16, :] = uu.reshape(4, 16, 256)
            tab_v[groups, at : at + 16, :] = vv.reshape(4, 16, 256)

    token = iota((256, 256), 0)
    other = iota((256, 256), 1)
    lane_group = lax.div(other, 16)

    def conv_tile(tile):
        part = slice(tile * 256, tile * 256 + 256)
        conv_ref[:, part] = jnp.zeros((256, 256), F32)

        @pl.loop(0, 16)
        def _(g):
            at = tile * 16 + g
            taps = jnp.where(token >= other, dot(tab_u[at], tab_v[at], 0, 0), 0.0).astype(BF16)
            masked = jnp.where(lane_group == g, z_ref[:, part].astype(F32), 0.0).astype(BF16)
            conv_ref[:, part] += dot(taps, masked)

    conv_tile(0)

    slab_decay = jnp.exp(-256.0 * rate_chan[...])
    for c in fz:
        c.wait_recv()
    first = zh == 0
    s_one = jnp.where(first, state_s[...], zin_s[...])
    s_two = jnp.where(first, zin_s[...], state_s[...])
    p_one = jnp.where(first, state_p[...], zin_p[...])
    p_two = jnp.where(first, zin_p[...], state_p[...])
    pair_s[...] = slab_decay * s_one + s_two
    pair_p[...] = slab_decay * (p_one + 256.0 * s_one) + p_two
    fx = []
    for i in range(3):
        fx.append(remote(pair_s, xin_s.at[i], fx_send.at[0, i], fx_recv.at[0, i], xpeer[i]))
        fx[-1].start()
    for i in range(3):
        fx.append(remote(pair_p, xin_p.at[i], fx_send.at[1, i], fx_recv.at[1, i], xpeer[i]))
        fx[-1].start()

    conv_tile(1)
    ag_step(1)

    @pl.loop(0, 4)
    def _(i):
        rows = pl.ds(pl.multiple_of(i * 64, 64), 64)
        at = (iota((64, 512), 0) + i * 64).astype(F32)
        rate, res = rate_row[...], res_row[...]
        f_high, f_low = split(res * jnp.exp(-rate * at))
        row_f[0, rows, :] = f_high
        row_f[1, rows, :] = f_low
        b_high, b_low = split(res * jnp.exp(-rate * (256.0 - at)))
        row_b[0, rows, :] = b_high
        row_b[1, rows, :] = b_low
        centre = at - 128.0
        up = jnp.exp(rate * centre)
        row_v[0, rows, :] = up.astype(BF16)
        row_v[1, rows, :] = (up * centre).astype(BF16)
        row_u[rows, :] = jnp.exp(-rate * centre)

    @pl.loop(0, 8)
    def _(i):
        rows = pl.ds(pl.multiple_of(i * 64, 64), 64)
        decay = jnp.exp(-rate_col[rows, :] * lane256)
        high, low = split(decay)
        e_q[0, rows, :] = high
        e_q[1, rows, :] = low
        e_q1[rows, :] = (decay * lane256).astype(BF16)

    for c in fx:
        c.wait_recv()
    sum_s = jnp.where(first, 0.0, zin_s[...])
    sum_p = jnp.where(first, 0.0, zin_p[...])
    for i in range(3):
        gap = 256.0 * (2 * i + zh).astype(F32)
        earlier = xx >= i + 1
        weight = jnp.exp(-gap * rate_chan[...])
        sum_s += jnp.where(earlier, weight * xin_s[i], 0.0)
        sum_p += jnp.where(earlier, weight * (xin_p[i] + gap * xin_s[i]), 0.0)
    in_s[...] = sum_s
    in_p[...] = sum_p

    def carried(rows, state, part):
        s_high, s_low = split(spread(state[:, part]))
        return (
            dot(rows[0, :, part], s_high) + dot(rows[1, :, part], s_high) + dot(rows[0, :, part], s_low)
        )

    for tile in range(2):
        part = slice(tile * 256, tile * 256 + 256)
        conv = conv_ref[:, part] + carried(row_f, in_s, part)
        conv_ref[:, part] = conv
        gated_ref[:, part] = (q_ref[:, part].astype(F32) * conv).astype(BF16)

    w_copy.wait()
    own_copy.wait()

    def w_block(j, a):
        return w_ref[pl.ds(pl.multiple_of((2 * j + a) * 512, 512), 512), :]

    def to_partner(j):
        return remote(pbuf.at[j], xbuf.at[j], p_send.at[j], p_recv.at[j], partner)

    @pl.loop(0, 4)
    def _(j):
        pbuf[j] = dot(gated_ref[...], w_block(j, 1 - core), 1, 1).astype(BF16)
        to_partner(j).start()

    @pl.loop(0, 4)
    def _(j):
        pacc[j] = dot(gated_ref[...], w_block(j, core), 1, 1)

    ag_step(2)

    @pl.loop(0, 4)
    def _(j):
        to_partner(j).wait_recv()
        pacc[j] += xbuf[j].astype(F32)

    def rs_right(j):
        return remote(snd_r.at[j], rec_l.at[j], rr_send.at[j], rr_recv.at[j], right)

    def rs_left(j):
        return remote(snd_l.at[j], rec_r.at[j], rl_send.at[j], rl_recv.at[j], left)

    def rs_step(m, end):
        jr, jl = 3 - m, m
        if end == 0:
            @pl.when(jnp.logical_and(jr > zl, zl == 0))
            def _():
                snd_r[jr] = pacc[jr].astype(BF16)
                rs_right(jr).start()

            @pl.when(jnp.logical_and(jl < zl, zl == 3))
            def _():
                snd_l[jl] = pacc[jl].astype(BF16)
                rs_left(jl).start()
        else:
            @pl.when(jnp.logical_and(jr > zl, zl > 0))
            def _():
                rs_right(jr).wait_recv()
                snd_r[jr] = (pacc[jr] + rec_l[jr].astype(F32)).astype(BF16)
                rs_right(jr).start()

            @pl.when(jnp.logical_and(jl < zl, zl < 3))
            def _():
                rs_left(jl).wait_recv()
                snd_l[jl] = (pacc[jl] + rec_r[jl].astype(F32)).astype(BF16)
                rs_left(jl).start()

    for m in range(3):
        rs_step(m, 0)

    ag_step(3)

    back_ref[...] = jnp.zeros((256, 512), F32)

    @pl.loop(0, 4)
    def _(j):
        back_ref[...] += dot(g_own[j], w_block(j, core))

    for j in range(4):
        ag_partner(d_ref, j).wait_recv()

    @pl.loop(0, 4)
    def _(j):
        back_ref[...] += dot(g_par[j], w_block(j, 1 - core))

    dconv_ref[...] = (q_ref[...].astype(F32) * back_ref[...]).astype(BF16)
    gq_ref[...] = (conv_ref[...] * back_ref[...]).astype(BF16)
    for tile in range(2):
        part = slice(tile * 256, tile * 256 + 256)
        dt = dconv_ref[:, part]
        state_q[:, part] = fold(dot(e_q[0, part, :], dt) + dot(e_q[1, part, :], dt))
        state_q1[:, part] = fold(dot(e_q1[part, :], dt))
    bz = remote(state_q, zin_q, fz_send.at[2], fz_recv.at[2], zpeer)
    bz.start()

    rs_step(0, 1)
    gsum[...] = jnp.zeros((8, 512), F32)

    def back_tile(tile):
        part = slice(tile * 256, tile * 256 + 256)
        dz_ref[:, part] = jnp.zeros((256, 256), F32)

        @pl.loop(0, 16)
        def _(g):
            at = tile * 16 + g
            taps = jnp.where(other >= token, dot(tab_v[at], tab_u[at], 0, 0), 0.0).astype(BF16)
            masked = jnp.where(lane_group == g, dconv_ref[:, part].astype(F32), 0.0).astype(BF16)
            dz_ref[:, part] += dot(taps, masked)
            mixed = jnp.where(token >= other, dot(masked, z_ref[:, part], 1, 1), 0.0).astype(BF16)
            first_sum = dot(mixed, row_v[0, :, part]) * row_u[:, part]
            second_sum = dot(mixed, row_v[1, :, part]) * row_u[:, part]
            centre = (token - 128).astype(F32)
            by_res = jnp.sum(first_sum.reshape(32, 8, 256), axis=0)
            by_rate = jnp.sum((first_sum * centre - second_sum).reshape(32, 8, 256), axis=0)
            mine = lax.div(iota((8, 256), 1), 16) == g
            gsum[:, part] += jnp.where(mine, by_res, 0.0)
            gout[:, part] += jnp.where(mine, by_rate, 0.0)

    gout[...] = jnp.zeros((8, 512), F32)
    back_tile(0)
    rs_step(1, 1)

    bz.wait_recv()
    q_one = jnp.where(first, state_q[...], zin_q[...])
    q_two = jnp.where(first, zin_q[...], state_q[...])
    pair_q[...] = q_one + slab_decay * q_two
    bx = []
    for i in range(3):
        bx.append(remote(pair_q, xin_q.at[i], bx_send.at[i], bx_recv.at[i], xpeer[i]))
        bx[-1].start()

    back_tile(1)
    rs_step(2, 1)

    fold_chan = sel_row
    by_res = dot_exact(state_q[...] * in_s[...], fold_chan, 1, 1)
    by_rate = dot_exact(state_q1[...] * in_s[...] + state_q[...] * in_p[...], fold_chan, 1, 1)
    flat_res = jnp.sum(gsum[...], axis=0, keepdims=True)
    flat_rate = jnp.sum(gout[...], axis=0, keepdims=True)
    by_res += dot_exact(jnp.where(own_row, flat_res, 0.0), fold_chan, 1, 1)
    by_rate += dot_exact(jnp.where(own_row, flat_rate, 0.0), fold_chan, 1, 1)
    gin_z[0] = jnp.zeros((32, 128), F32)
    gin_z[0, 0:16, 0:32] = by_res
    gin_z[0, 16:32, 0:32] = by_rate

    def exchange(src, dst, at, peers):
        copies = []
        for i, dev in enumerate(peers):
            copies.append(remote(src, dst.at[i], gs_send.at[at + i], gs_recv.at[at + i], dev))
            copies[-1].start()
        return copies

    started = exchange(gin_z.at[0], gin_y, 0, ypeer)

    for c in bx:
        c.wait_recv()
    sum_q = jnp.where(first, zin_q[...], 0.0)
    for i in range(3):
        steps = 4 - (i + 1)
        later = xx + steps <= 3
        gap = 256.0 * (2 * (steps - 1) + 1 - zh).astype(F32)
        sum_q += jnp.where(later, jnp.exp(-gap * rate_chan[...]) * xin_q[i], 0.0)
    in_q[...] = sum_q
    for tile in range(2):
        part = slice(tile * 256, tile * 256 + 256)
        dz = dz_ref[:, part] + carried(row_b, in_q, part)
        gv_ref[:, part] = (dz * k_ref[:, part].astype(F32)).astype(BF16)
        gk_ref[:, part] = (dz * v_ref[:, part].astype(F32)).astype(BF16)

    for c in started:
        c.wait_recv()
    gin_z[1] = gin_z[0] + gin_y[0] + gin_y[1] + gin_y[2]
    more = exchange(gin_z.at[1], gin_x, 3, xpeer)
    for c in more:
        c.wait_recv()
    started += more
    gin_z[2] = gin_z[1] + gin_x[0] + gin_x[1] + gin_x[2]
    last = remote(gin_z.at[2], gin_z.at[3], gs_send.at[6], gs_recv.at[6], zpeer)
    last.start()

    @pl.when(has_left)
    def _():
        rs_right(zl).wait_recv()
        pacc[zl] += rec_l[zl].astype(F32)

    @pl.when(has_right)
    def _():
        rs_left(zl).wait_recv()
        pacc[zl] += rec_r[zl].astype(F32)

    out_ref[...] = pacc[zl].astype(BF16)

    last.wait_recv()
    total = gin_z[2] + gin_z[3]
    gres_ref[...] = total[0:16, 0:32]
    grate_ref[...] = -res_ref[...] * total[16:32, 0:32]

    for c in fz + fx + bx + [bz, last] + started:
        c.wait_send()
    ag_drain()
    for j in range(4):
        to_partner(j).wait_send()

        @pl.when(j > zl)
        def _():
            rs_right(j).wait_send()

        @pl.when(j < zl)
        def _():
            rs_left(j).wait_send()


def per_device(values_in, keys_in, query_in, cotangent, out_weight, residues, rates):
    vm = pltpu.VMEM
    dma = pltpu.SemaphoreType.DMA
    act = jax.ShapeDtypeStruct((256, 512), BF16)
    par = jax.ShapeDtypeStruct((16, 32), F32)
    spec = pl.BlockSpec(memory_space=pltpu.VMEM)
    blocks = lambda: vm((4, 256, 512), BF16)
    state = lambda: vm((16, 512), F32)
    states = lambda: vm((3, 16, 512), F32)
    scratch = [
        vm((4096, 512), BF16), dma, dma,
        vm((512, 1), F32), vm((512, 1), F32), vm((1, 512), F32), vm((1, 512), F32), state(),
        vm((32, 48, 256), BF16), vm((32, 48, 256), BF16),
        vm((2, 512, 256), BF16), vm((512, 256), BF16), vm((2, 512, 256), BF16), vm((512, 256), BF16),
        vm((2, 256, 512), BF16), vm((2, 256, 512), BF16), vm((2, 256, 512), BF16), vm((256, 512), F32),
        vm((256, 512), BF16), vm((256, 512), F32), vm((256, 512), BF16), vm((256, 512), BF16),
        vm((256, 512), F32), vm((256, 512), F32),
        state(), state(), state(), state(), state(), state(), states(), states(), state(), state(),
        state(), state(), state(), state(), states(), state(),
        blocks(), blocks(), vm((4, 256, 512), F32), blocks(), blocks(), blocks(), blocks(), blocks(), blocks(),
        vm((8, 512), F32), vm((8, 512), F32),
        vm((3, 32, 128), F32), vm((3, 32, 128), F32), vm((4, 32, 128), F32),
        dma((2, 3)), dma((4,)), dma((4,)), dma((4,)),
        dma((3,)), dma((3,)), dma((2, 3)), dma((2, 3)), dma((3,)), dma((3,)),
        dma((4,)), dma((4,)), dma((4,)), dma((4,)), dma((4,)), dma((4,)), dma((7,)), dma((7,)),
    ]
    out, gv, gk, gq, gres, grate = pl.pallas_call(
        kernel,
        out_shape=(act, act, act, act, par, par),
        in_specs=[spec, spec, spec, spec, pl.BlockSpec(memory_space=pl.ANY), spec, spec],
        out_specs=(spec,) * 6,
        scratch_shapes=scratch,
        compiler_params=pltpu.CompilerParams(
            collective_id=0, has_side_effects=True, vmem_limit_bytes=60 * 1024 * 1024
        ),
        name="hyena",
    )(values_in[0], keys_in[0], query_in[0], cotangent[0], out_weight, rates, residues)
    return out[None], gv[None], gk[None], gq[None], gres, grate


def solution(mesh):
    act = P("rep", "ctx", "chan")
    par = P(None, "chan")
    return jax.shard_map(
        per_device,
        mesh=mesh,
        in_specs=(act, act, act, act, par, par, par),
        out_specs=(act, act, act, act, par, par),
        check_vma=False,
    )
```

time: 588 us -> 90.1 us (0.15)
  the two profiles are of different devices: /device:TPU:96 before, /device:TPU:32 now
where the time goes in v1:
time: 90.1 us; the launch traced here: 89.8 us
  Pallas kernels  79.9 us (89%)
  local copies, waits for them, and re-layouts  9.26 us (10%)
    pallas_call x1, Pallas kernels, per_device(): pl.pallas_call(kernel, out_shape=(act, act, act, act, par, par), in_specs...  79.9 us
    unnamed x6, local copies, waits for them, and re-layouts  9.26 us

profile of v1, /device:TPU:32, one launch (start us, length us, event | category | flops | bytes accessed | tf_op | source)
XLA Modules:
  0.0 89.8 jit_solution(8481613844216347787)
XLA Ops:
  0.6 79.9 %hyena.1 = (bf16[256,512]{1,0:T(8,128)(2,1)}, bf16[256,512]{1,0:T(8,128)(2,1)}, bf16[256,512]{1,0:T(8,128)(2,1)}, bf16[256,512]{1,0:T(8,128)(2,1)}, f32[16,32]{1,0:T(8,128)}, /*index=5*/f32[16,32]{1,0:T(8,128)}) custom-call(bf16[256,512]{1,0:T(8,128)(2,1)} %bitcast.8, bf16[256,512]{1,0:T(8,128)(2,1)} %bitcast.9, bf16[256,512]{1,0:T(8,128)(2,1)} %bitcast.10, ...), custom_call_target="tpu_custom_call" | custom-call | tf_op jit(solution)/shard_map/hyena/pallas_call | solution.py:516
  80.6 1.7 %copy.19 = bf16[1,256,512]{2,1,0:T(8,128)(2,1)} copy(bf16[1,256,512]{2,1,0:T(8,128)(2,1)} %bitcast.15) | data formatting | bytes 524288
  82.2 1.7 %copy.20 = bf16[1,256,512]{2,1,0:T(8,128)(2,1)} copy(bf16[1,256,512]{2,1,0:T(8,128)(2,1)} %bitcast.14) | data formatting | bytes 524288
  83.9 1.7 %copy.21 = bf16[1,256,512]{2,1,0:T(8,128)(2,1)} copy(bf16[1,256,512]{2,1,0:T(8,128)(2,1)} %bitcast.13) | data formatting | bytes 524288
  85.6 1.7 %copy.22 = bf16[1,256,512]{2,1,0:T(8,128)(2,1)} copy(bf16[1,256,512]{2,1,0:T(8,128)(2,1)} %bitcast.12) | data formatting | bytes 524288
  87.2 1.3 %copy.23 = f32[16,32]{1,0:T(8,128)} copy(f32[16,32]{1,0:T(8,128)} %get-tuple-element.28) | data formatting | bytes 4096
  88.5 1.3 %copy.24 = f32[16,32]{1,0:T(8,128)} copy(f32[16,32]{1,0:T(8,128)} %get-tuple-element.29) | data formatting | bytes 4096

commit v2 on v1

v2 whole, which is shorter than its diff:
```python
import functools

import jax
import jax.numpy as jnp
from jax import lax
from jax.experimental import pallas as pl
from jax.experimental.pallas import tpu as pltpu
from jax.sharding import PartitionSpec as P

GROUP = 16
F32 = jnp.float32
BF16 = jnp.bfloat16
MESH = pl.DeviceIdType.MESH


def iota(shape, axis):
    return lax.broadcasted_iota(jnp.int32, shape, axis)


def dot(a, b, ca=1, cb=0):
    return lax.dot_general(a, b, (((ca,), (cb,)), ((), ())), preferred_element_type=F32)


def dot_exact(a, b, ca=1, cb=0):
    return lax.dot_general(
        a, b, (((ca,), (cb,)), ((), ())), precision=lax.Precision.HIGHEST, preferred_element_type=F32
    )


def split(a):
    high = a.astype(BF16)
    return high, (a - high.astype(F32)).astype(BF16)


def kernel(
    v_ref, k_ref, q_ref, d_ref, w_hbm, rates_ref, res_ref,
    out_ref, gv_ref, gk_ref, gq_ref, gres_ref, grate_ref,
    w_ref, w_sem, own_sem,
    rate_col, res_col, rate_row, res_row, rate_chan,
    tab_u, tab_v, tab_m, col_u, taps_back, z_mask, prod_res, prod_rate,
    e_s, e_p, e_q, e_q1, row_f, row_b,
    z_ref, conv_ref, gated_ref, dconv_ref, back_ref, dz_ref,
    state_s, state_p, pair_s, pair_p, zin_s, zin_p, xin_s, xin_p, in_s, in_p,
    state_q, state_q1, pair_q, zin_q, xin_q, in_q,
    g_own, g_par, pacc, pbuf, xbuf, snd_r, snd_l, rec_l, rec_r,
    gsum, gin_y, gin_c,
    ag_send, ag_recv, agp_send, agp_recv,
    fz_send, fz_recv, fx_send, fx_recv, bx_send, bx_recv,
    p_send, p_recv, rr_send, rr_recv, rl_send, rl_recv, gs_send, gs_recv,
):
    chan = lax.axis_index("chan")
    ctx = lax.axis_index("ctx")
    rep = lax.axis_index("rep")
    core, zl = lax.rem(chan, 2), lax.div(chan, 2)
    zh, xx = lax.rem(ctx, 2), lax.div(ctx, 2)
    has_left, has_right = zl > 0, zl < 3
    left, right, partner = {"chan": chan - 2}, {"chan": chan + 2}, {"chan": chan + 1 - 2 * core}
    zpeer = {"ctx": ctx + 1 - 2 * zh}
    xpeer = [{"ctx": lax.rem(xx + i, 4) * 2 + zh} for i in (1, 2, 3)]
    cpeer = [{"ctx": lax.rem(ctx + i, 8)} for i in range(1, 8)]
    ypeer = [{"rep": lax.rem(rep + i, 4)} for i in (1, 2, 3)]

    def remote(src, dst, ssem, rsem, dev):
        return pltpu.make_async_remote_copy(
            src_ref=src, dst_ref=dst, send_sem=ssem, recv_sem=rsem, device_id=dev, device_id_type=MESH
        )

    w_copy = pltpu.make_async_copy(w_hbm, w_ref, w_sem)
    w_copy.start()
    own_copy = pltpu.make_async_copy(d_ref, g_own.at[zl], own_sem)
    own_copy.start()
    barrier = pltpu.get_barrier_semaphore()
    for dev in [partner] + cpeer + ypeer:
        pl.semaphore_signal(barrier, inc=1, device_id=dev, device_id_type=MESH)

    @pl.when(has_left)
    def _():
        pl.semaphore_signal(barrier, inc=1, device_id=left, device_id_type=MESH)

    @pl.when(has_right)
    def _():
        pl.semaphore_signal(barrier, inc=1, device_id=right, device_id_type=MESH)

    sel_row = jnp.where(lax.div(iota((32, 512), 1), 16) == iota((32, 512), 0), 1.0, 0.0).astype(F32)
    own_row = lax.rem(iota((16, 512), 1), 16) == iota((16, 512), 0)
    for src, col, row in ((rates_ref, rate_col, rate_row), (res_ref, res_col, res_row)):
        flat = dot_exact(src[...], sel_row)
        line = jnp.sum(jnp.where(own_row, flat, 0.0), axis=0, keepdims=True)
        row[...] = line
        col[...] = jnp.transpose(jnp.broadcast_to(line, (128, 512)))
        if src is rates_ref:
            rate_chan[...] = flat

    def wide(ref, rows):
        return jnp.concatenate([ref[rows, :], ref[rows, :]], axis=1)

    lane256 = iota((64, 256), 1).astype(F32)

    @pl.loop(0, 8)
    def _(i):
        rows = pl.ds(pl.multiple_of(i * 64, 64), 64)
        rate = wide(rate_col, rows)
        left_over = 256.0 - lane256
        decay = jnp.exp(-rate * left_over)
        high, low = split(decay)
        e_s[0, rows, :] = high
        e_s[1, rows, :] = low
        e_p[rows, :] = (decay * left_over).astype(BF16)

    pl.semaphore_wait(barrier, 11 + jnp.where(has_left, 1, 0) + jnp.where(has_right, 1, 0))

    def half(h):
        return pl.ds(h * 128, 128)

    def ag_right(src_ref, src, m, h):
        return remote(
            src_ref.at[half(h)], g_own.at[src, half(h)], ag_send.at[0, m, h], ag_recv.at[src, h], right
        )

    def ag_left(src_ref, src, m, h):
        return remote(
            src_ref.at[half(h)], g_own.at[src, half(h)], ag_send.at[1, m, h], ag_recv.at[src, h], left
        )

    def ag_partner(src_ref, src, h):
        return remote(
            src_ref.at[half(h)], g_par.at[src, half(h)], agp_send.at[src, h], agp_recv.at[src, h], partner
        )

    for h in range(2):
        @pl.when(has_right)
        def _():
            ag_right(d_ref, zl, 0, h).start()

        @pl.when(has_left)
        def _():
            ag_left(d_ref, zl, 0, h).start()

    for h in range(2):
        ag_partner(d_ref, zl, h).start()

    def ag_step(m, h):
        src_l, src_r = zl - m, zl + m

        @pl.when(src_l >= 0)
        def _():
            ag_right(g_own.at[src_l], src_l, 0, h).wait_recv()

            if m < 3:
                @pl.when(has_right)
                def _():
                    ag_right(g_own.at[src_l], src_l, m, h).start()

            ag_partner(g_own.at[src_l], src_l, h).start()

        @pl.when(src_r <= 3)
        def _():
            ag_left(g_own.at[src_r], src_r, 0, h).wait_recv()

            if m < 3:
                @pl.when(has_left)
                def _():
                    ag_left(g_own.at[src_r], src_r, m, h).start()

            ag_partner(g_own.at[src_r], src_r, h).start()

    def ag_drain():
        for h in range(2):
            for m in range(3):
                @pl.when(jnp.logical_and(has_right, zl - m >= 0))
                def _():
                    ag_right(d_ref, zl, m, h).wait_send()

                @pl.when(jnp.logical_and(has_left, zl + m <= 3))
                def _():
                    ag_left(d_ref, zl, m, h).wait_send()

            for j in range(4):
                ag_partner(d_ref, j, h).wait_send()

    z_ref[...] = (k_ref[...].astype(F32) * v_ref[...].astype(F32)).astype(BF16)
    own_block = lax.div(iota((256, 256), 0), 16) == lax.div(iota((256, 256), 1), 16)

    def fold(a):
        return jnp.sum(jnp.where(own_block, a, 0.0).reshape(16, 16, 256), axis=0)

    def spread(s):
        return jnp.where(own_block, jnp.broadcast_to(s[None], (16, 16, 256)).reshape(256, 256), 0.0)

    for tile in range(2):
        part = slice(tile * 256, tile * 256 + 256)
        zt = z_ref[:, part]
        state_s[:, part] = fold(dot(e_s[0, part, :], zt) + dot(e_s[1, part, :], zt))
        state_p[:, part] = fold(dot(e_p[part, :], zt))

    fz = [
        remote(state_s, zin_s, fz_send.at[0], fz_recv.at[0], zpeer),
        remote(state_p, zin_p, fz_send.at[1], fz_recv.at[1], zpeer),
    ]
    for c in fz:
        c.start()

    @pl.loop(0, 8)
    def _(i):
        rows = pl.ds(pl.multiple_of(i * 64, 64), 64)
        groups = pl.ds(i * 4, 4)
        rate, res = wide(rate_col, rows), wide(res_col, rows)
        centre = lane256 - 128.0
        fall, rise = jnp.exp(-rate * centre), jnp.exp(rate * centre)
        u_high, u_low = split(res * fall)
        v_high, v_low = split(rise)
        for at, uu, vv in ((0, u_high, v_high), (16, u_high, v_low), (32, u_low, v_high)):
            tab_u[groups, at : at + 16, :] = uu.reshape(4, 16, 256)
            tab_v[groups, at : at + 16, :] = vv.reshape(4, 16, 256)
        tab_m[groups, 0:16, :] = v_high.reshape(4, 16, 256)
        tab_m[groups, 16:32, :] = (rise * centre).astype(BF16).reshape(4, 16, 256)
        col_u[rows, :] = fall

    token = iota((256, 256), 0)
    other = iota((256, 256), 1)
    lane_group = lax.div(other, 16)

    def conv_tile(tile, low, high):
        part = slice(tile * 256, tile * 256 + 256)

        @pl.loop(low, high)
        def _(i):
            for g in (2 * i, 2 * i + 1):
                at = tile * 16 + g
                taps = jnp.where(token >= other, dot(tab_u[at], tab_v[at], 0, 0), 0.0).astype(BF16)
                conv_ref[:, part] = jnp.where(
                    lane_group == g, dot(taps, z_ref[:, part]), conv_ref[:, part]
                )

    def taps_tile(tile):
        part = slice(tile * 256, tile * 256 + 256)

        @pl.loop(0, 8)
        def _(i):
            for g in (2 * i, 2 * i + 1):
                at = tile * 16 + g
                taps = jnp.where(other >= token, dot(tab_v[at], tab_u[at], 0, 0), 0.0)
                taps_back[at] = taps.astype(BF16)
                z_mask[at] = jnp.where(lane_group == g, z_ref[:, part].astype(F32), 0.0).astype(BF16)

    conv_tile(0, 0, 8)

    slab_decay = jnp.exp(-256.0 * rate_chan[...])
    for c in fz:
        c.wait_recv()
    first = zh == 0
    s_one = jnp.where(first, state_s[...], zin_s[...])
    s_two = jnp.where(first, zin_s[...], state_s[...])
    p_one = jnp.where(first, state_p[...], zin_p[...])
    p_two = jnp.where(first, zin_p[...], state_p[...])
    pair_s[...] = slab_decay * s_one + s_two
    pair_p[...] = slab_decay * (p_one + 256.0 * s_one) + p_two
    fx = []
    for i in range(3):
        fx.append(remote(pair_s, xin_s.at[i], fx_send.at[0, i], fx_recv.at[0, i], xpeer[i]))
        fx[-1].start()
    for i in range(3):
        fx.append(remote(pair_p, xin_p.at[i], fx_send.at[1, i], fx_recv.at[1, i], xpeer[i]))
        fx[-1].start()

    ag_step(1, 0)
    conv_tile(1, 0, 4)
    ag_step(1, 1)
    conv_tile(1, 4, 8)

    @pl.loop(0, 4)
    def _(i):
        rows = pl.ds(pl.multiple_of(i * 64, 64), 64)
        at = (iota((64, 512), 0) + i * 64).astype(F32)
        rate, res = rate_row[...], res_row[...]
        f_high, f_low = split(res * jnp.exp(-rate * at))
        row_f[0, rows, :] = f_high
        row_f[1, rows, :] = f_low
        b_high, b_low = split(res * jnp.exp(-rate * (256.0 - at)))
        row_b[0, rows, :] = b_high
        row_b[1, rows, :] = b_low

    @pl.loop(0, 8)
    def _(i):
        rows = pl.ds(pl.multiple_of(i * 64, 64), 64)
        decay = jnp.exp(-wide(rate_col, rows) * lane256)
        high, low = split(decay)
        e_q[0, rows, :] = high
        e_q[1, rows, :] = low
        e_q1[rows, :] = (decay * lane256).astype(BF16)

    ag_step(2, 0)
    for c in fx:
        c.wait_recv()
    sum_s = jnp.where(first, 0.0, zin_s[...])
    sum_p = jnp.where(first, 0.0, zin_p[...])
    for i in range(3):
        gap = 256.0 * (2 * i + zh).astype(F32)
        earlier = xx >= i + 1
        weight = jnp.exp(-gap * rate_chan[...])
        sum_s += jnp.where(earlier, weight * xin_s[i], 0.0)
        sum_p += jnp.where(earlier, weight * (xin_p[i] + gap * xin_s[i]), 0.0)
    in_s[...] = sum_s
    in_p[...] = sum_p

    def carried(rows, state, part):
        s_high, s_low = split(spread(state[:, part]))
        return (
            dot(rows[0, :, part], s_high) + dot(rows[1, :, part], s_high) + dot(rows[0, :, part], s_low)
        )

    for tile in range(2):
        part = slice(tile * 256, tile * 256 + 256)
        conv = conv_ref[:, part] + carried(row_f, in_s, part)
        conv_ref[:, part] = conv
        gated_ref[:, part] = (q_ref[:, part].astype(F32) * conv).astype(BF16)

    w_copy.wait()
    own_copy.wait()

    def w_block(j, a):
        return w_ref[pl.ds(pl.multiple_of((2 * j + a) * 512, 512), 512), :]

    def to_partner(j):
        return remote(pbuf.at[j], xbuf.at[j], p_send.at[j], p_recv.at[j], partner)

    @pl.loop(0, 4)
    def _(j):
        pbuf[j] = dot(gated_ref[...], w_block(j, 1 - core), 1, 1).astype(BF16)
        to_partner(j).start()

    @pl.loop(0, 4)
    def _(j):
        pacc[j] = dot(gated_ref[...], w_block(j, core), 1, 1)

    @pl.loop(0, 4)
    def _(j):
        to_partner(j).wait_recv()
        pacc[j] += xbuf[j].astype(F32)

    def rs_right(j, h):
        return remote(snd_r.at[j, half(h)], rec_l.at[j, half(h)], rr_send.at[j, h], rr_recv.at[j, h], right)

    def rs_left(j, h):
        return remote(snd_l.at[j, half(h)], rec_r.at[j, half(h)], rl_send.at[j, h], rl_recv.at[j, h], left)

    def rs_first(m, h):
        jr, jl = 3 - m, m

        @pl.when(zl == 0)
        def _():
            snd_r[jr, half(h)] = pacc[jr, half(h)].astype(BF16)
            rs_right(jr, h).start()

        @pl.when(zl == 3)
        def _():
            snd_l[jl, half(h)] = pacc[jl, half(h)].astype(BF16)
            rs_left(jl, h).start()

    def rs_hop(m, h):
        jr, jl = 3 - m, m

        @pl.when(jnp.logical_and(jr > zl, zl > 0))
        def _():
            rs_right(jr, h).wait_recv()
            snd_r[jr, half(h)] = (pacc[jr, half(h)] + rec_l[jr, half(h)].astype(F32)).astype(BF16)
            rs_right(jr, h).start()

        @pl.when(jnp.logical_and(jl < zl, zl < 3))
        def _():
            rs_left(jl, h).wait_recv()
            snd_l[jl, half(h)] = (pacc[jl, half(h)] + rec_r[jl, half(h)].astype(F32)).astype(BF16)
            rs_left(jl, h).start()

    for m in range(3):
        for h in range(2):
            rs_first(m, h)

    def back_own(j):
        back_ref[...] += dot(g_own[j], w_block(j, core))

    def back_par(j):
        for h in range(2):
            ag_partner(d_ref, j, h).wait_recv()
        back_ref[...] += dot(g_par[j], w_block(j, 1 - core))

    def both_sides(act, m):
        @pl.when(zl - m >= 0)
        def _():
            act(zl - m)

        @pl.when(zl + m <= 3)
        def _():
            act(zl + m)

    ag_step(2, 1)
    back_ref[...] = dot(g_own[zl], w_block(zl, core))
    back_par(zl)
    taps_tile(0)
    rs_hop(0, 0)
    both_sides(back_own, 1)
    both_sides(back_par, 1)
    ag_step(3, 0)
    rs_hop(0, 1)
    taps_tile(1)
    both_sides(back_own, 2)
    both_sides(back_par, 2)
    ag_step(3, 1)
    both_sides(back_own, 3)
    rs_hop(1, 0)
    both_sides(back_par, 3)

    dconv_ref[...] = (q_ref[...].astype(F32) * back_ref[...]).astype(BF16)
    for tile in range(2):
        part = slice(tile * 256, tile * 256 + 256)
        dt = dconv_ref[:, part]
        state_q[:, part] = fold(dot(e_q[0, part, :], dt) + dot(e_q[1, part, :], dt))
    bz = remote(state_q, zin_q, fz_send.at[2], fz_recv.at[2], zpeer)
    bz.start()
    rs_hop(1, 1)
    for tile in range(2):
        part = slice(tile * 256, tile * 256 + 256)
        state_q1[:, part] = fold(dot(e_q1[part, :], dconv_ref[:, part]))

    centre16 = (iota((16, 256), 1) - 128).astype(F32)

    def mixed_tile(tile):
        part = slice(tile * 256, tile * 256 + 256)

        @pl.loop(0, 4)
        def _(i):
            for k in range(4):
                at = tile * 16 + 4 * i + k
                mixed = jnp.where(token >= other, dot(dconv_ref[:, part], z_mask[at], 1, 1), 0.0)
                sums = dot(tab_m[at], mixed.astype(BF16), 1, 1)
                rows = pl.ds(pl.multiple_of(at * 16, 16), 16)
                fall = col_u[rows, :]
                prod_res[rows, :] = fall * sums[0:16]
                prod_rate[rows, :] = fall * (centre16 * sums[0:16] - sums[16:32])

    def dz_tile(tile):
        part = slice(tile * 256, tile * 256 + 256)

        @pl.loop(0, 8)
        def _(i):
            for g in (2 * i, 2 * i + 1):
                at = tile * 16 + g
                dz_ref[:, part] = jnp.where(
                    lane_group == g, dot(taps_back[at], dconv_ref[:, part]), dz_ref[:, part]
                )

    mixed_tile(0)
    rs_hop(2, 0)
    mixed_tile(1)
    rs_hop(2, 1)

    pick_pole = jnp.where(own_row, 1.0, 0.0).astype(F32)
    pick_group = lax.div(iota((512, 32), 0), 16) == iota((512, 32), 1)

    def param_sum(prod, cross):
        column = jnp.sum(prod[...], axis=1, keepdims=True)
        return dot_exact(pick_pole, jnp.where(pick_group, column, 0.0)) + dot_exact(cross, sel_row, 1, 1)

    gsum[0] = jnp.zeros((32, 128), F32)
    gsum[0, 0:16, 0:32] = param_sum(prod_res, state_q[...] * in_s[...])
    gsum[0, 16:32, 0:32] = param_sum(prod_rate, state_q1[...] * in_s[...] + state_q[...] * in_p[...])

    def exchange(src, dst, at, peers):
        copies = []
        for i, dev in enumerate(peers):
            copies.append(remote(src, dst.at[i], gs_send.at[at + i], gs_recv.at[at + i], dev))
            copies[-1].start()
        return copies

    started = exchange(gsum.at[0], gin_y, 0, ypeer)
    dz_tile(0)

    bz.wait_recv()
    q_one = jnp.where(first, state_q[...], zin_q[...])
    q_two = jnp.where(first, zin_q[...], state_q[...])
    pair_q[...] = q_one + slab_decay * q_two
    bx = []
    for i in range(3):
        bx.append(remote(pair_q, xin_q.at[i], bx_send.at[i], bx_recv.at[i], xpeer[i]))
        bx[-1].start()

    for c in started:
        c.wait_recv()
    gsum[1] = gsum[0] + gin_y[0] + gin_y[1] + gin_y[2]
    last = exchange(gsum.at[1], gin_c, 3, cpeer)

    dz_tile(1)
    gq_ref[...] = (conv_ref[...] * back_ref[...]).astype(BF16)

    for c in bx:
        c.wait_recv()
    sum_q = jnp.where(first, zin_q[...], 0.0)
    for i in range(3):
        steps = 4 - (i + 1)
        later = xx + steps <= 3
        gap = 256.0 * (2 * (steps - 1) + 1 - zh).astype(F32)
        sum_q += jnp.where(later, jnp.exp(-gap * rate_chan[...]) * xin_q[i], 0.0)
    in_q[...] = sum_q
    for tile in range(2):
        part = slice(tile * 256, tile * 256 + 256)
        dz = dz_ref[:, part] + carried(row_b, in_q, part)
        gv_ref[:, part] = (dz * k_ref[:, part].astype(F32)).astype(BF16)
        gk_ref[:, part] = (dz * v_ref[:, part].astype(F32)).astype(BF16)

    for c in last:
        c.wait_recv()
    total = gsum[1]
    for i in range(7):
        total += gin_c[i]
    gres_ref[...] = total[0:16, 0:32]
    grate_ref[...] = -res_ref[...] * total[16:32, 0:32]

    for h in range(2):
        @pl.when(has_left)
        def _():
            rs_right(zl, h).wait_recv()
            pacc[zl, half(h)] += rec_l[zl, half(h)].astype(F32)

        @pl.when(has_right)
        def _():
            rs_left(zl, h).wait_recv()
            pacc[zl, half(h)] += rec_r[zl, half(h)].astype(F32)

    out_ref[...] = pacc[zl].astype(BF16)

    for c in fz + fx + bx + [bz] + started + last:
        c.wait_send()
    ag_drain()
    for j in range(4):
        to_partner(j).wait_send()
        for h in range(2):
            @pl.when(j > zl)
            def _():
                rs_right(j, h).wait_send()

            @pl.when(j < zl)
            def _():
                rs_left(j, h).wait_send()


def hand_over(*refs):
    half_way = len(refs) // 2
    for src, dst in zip(refs[:half_way], refs[half_way:]):
        dst[...] = src[...]


def per_device(values_in, keys_in, query_in, cotangent, out_weight, residues, rates):
    vm = pltpu.VMEM
    dma = pltpu.SemaphoreType.DMA
    act = jax.ShapeDtypeStruct((256, 512), BF16)
    par = jax.ShapeDtypeStruct((16, 32), F32)
    spec = pl.BlockSpec(memory_space=pltpu.VMEM)
    blocks = lambda: vm((4, 256, 512), BF16)
    state = lambda: vm((16, 512), F32)
    states = lambda: vm((3, 16, 512), F32)
    scratch = [
        vm((4096, 512), BF16), dma, dma,
        vm((512, 128), F32), vm((512, 128), F32), vm((1, 512), F32), vm((1, 512), F32), state(),
        vm((32, 48, 256), BF16), vm((32, 48, 256), BF16), vm((32, 32, 256), BF16), vm((512, 256), F32),
        vm((32, 256, 256), BF16), vm((32, 256, 256), BF16), vm((512, 256), F32), vm((512, 256), F32),
        vm((2, 512, 256), BF16), vm((512, 256), BF16), vm((2, 512, 256), BF16), vm((512, 256), BF16),
        vm((2, 256, 512), BF16), vm((2, 256, 512), BF16),
        vm((256, 512), BF16), vm((256, 512), F32), vm((256, 512), BF16), vm((256, 512), BF16),
        vm((256, 512), F32), vm((256, 512), F32),
        state(), state(), state(), state(), state(), state(), states(), states(), state(), state(),
        state(), state(), state(), state(), states(), state(),
        blocks(), blocks(), vm((4, 256, 512), F32), blocks(), blocks(), blocks(), blocks(), blocks(), blocks(),
        vm((2, 32, 128), F32), vm((3, 32, 128), F32), vm((7, 32, 128), F32),
        dma((2, 3, 2)), dma((4, 2)), dma((4, 2)), dma((4, 2)),
        dma((3,)), dma((3,)), dma((2, 3)), dma((2, 3)), dma((3,)), dma((3,)),
        dma((4,)), dma((4,)), dma((4, 2)), dma((4, 2)), dma((4, 2)), dma((4, 2)), dma((10,)), dma((10,)),
    ]
    shapes = (act, act, act, act, par, par)
    results = pl.pallas_call(
        kernel,
        out_shape=shapes,
        in_specs=[spec, spec, spec, spec, pl.BlockSpec(memory_space=pl.ANY), spec, spec],
        out_specs=(spec,) * 6,
        scratch_shapes=scratch,
        compiler_params=pltpu.CompilerParams(
            collective_id=0, has_side_effects=True, vmem_limit_bytes=60 * 1024 * 1024
        ),
        name="hyena",
    )(values_in[0], keys_in[0], query_in[0], cotangent[0], out_weight, rates, residues)
    out, gv, gk, gq, gres, grate = pl.pallas_call(
        hand_over, out_shape=shapes, in_specs=[spec] * 6, out_specs=(spec,) * 6, name="results"
    )(*results)
    return out[None], gv[None], gk[None], gq[None], gres, grate


def solution(mesh):
    act = P("rep", "ctx", "chan")
    par = P(None, "chan")
    return jax.shard_map(
        per_device,
        mesh=mesh,
        in_specs=(act, act, act, act, par, par, par),
        out_specs=(act, act, act, act, par, par),
        check_vma=False,
    )
```

time: 90.1 us -> 80.2 us (0.89)
  local copies, waits for them, and re-layouts: 9.26 us -> 0 us
    unnamed x6 -> x0, local copies, waits for them, and re-layouts: 9.26 us -> none
    pallas_call x1 -> x2, Pallas kernels: 79.9 us -> 79.5 us  [the longest x1 77.3 us: per_device(): pl.pallas_call(kernel, out_shape=shapes, in_specs=[spec, spec, spec, spec...]
where the time goes in v2:
time: 80.2 us; the launch traced here: 80.1 us
  Pallas kernels  79.5 us (99%)
    pallas_call x1, Pallas kernels, per_device(): pl.pallas_call(kernel, out_shape=shapes, in_specs=[spec, spec, spec, spec...  77.3 us
    pallas_call x1, Pallas kernels, per_device(): pl.pallas_call(hand_over, out_shape=shapes, in_specs=[spec] * 6, out_spec...  2.18 us

profile of v2, /device:TPU:32, one launch (start us, length us, event | category | flops | bytes accessed | tf_op | source)
XLA Modules:
  0.0 80.1 jit_solution(16630269601297218565)
XLA Ops:
  0.6 77.3 %hyena.1 = (bf16[256,512]{1,0:T(8,128)(2,1)}, bf16[256,512]{1,0:T(8,128)(2,1)}, bf16[256,512]{1,0:T(8,128)(2,1)}, bf16[256,512]{1,0:T(8,128)(2,1)}, f32[16,32]{1,0:T(8,128)}, /*index=5*/f32[16,32]{1,0:T(8,128)}) custom-call(bf16[256,512]{1,0:T(8,128)(2,1)} %bitcast.8, bf16[256,512]{1,0:T(8,128)(2,1)} %bitcast.9, bf16[256,512]{1,0:T(8,128)(2,1)} %bitcast.10, ...), custom_call_target="tpu_custom_call" | custom-call | tf_op jit(solution)/shard_map/hyena/pallas_call | solution.py:579
  77.9 2.2 %results.1 = (bf16[256,512]{1,0:T(8,128)(2,1)}, bf16[256,512]{1,0:T(8,128)(2,1)}, bf16[256,512]{1,0:T(8,128)(2,1)}, bf16[256,512]{1,0:T(8,128)(2,1)}, f32[16,32]{1,0:T(8,128)}, /*index=5*/f32[16,32]{1,0:T(8,128)}) custom-call(bf16[256,512]{1,0:T(8,128)(2,1)} %get-tuple-element.18.refs_0_, bf16[256,512]{1,0:T(8,128)(2,1)} %get-tuple-element.19.refs_1_, ...), custom_call_target="tpu_custom_call" | custom-call | tf_op jit(solution)/shard_map/results/pallas_call | solution.py:590

commit v3 on v2

--- a/solution.py
+++ b/solution.py
@@ -42,19 +42,21 @@
     z_ref, conv_ref, gated_ref, dconv_ref, back_ref, dz_ref,
     state_s, state_p, pair_s, pair_p, zin_s, zin_p, xin_s, xin_p, in_s, in_p,
     state_q, state_q1, pair_q, zin_q, xin_q, in_q,
-    g_own, g_par, pacc, pbuf, xbuf, snd_r, snd_l, rec_l, rec_r,
+    g_own, g_par, pacc, pbuf, xbuf, snd_n, rec_n, snd_f, rec_f,
     gsum, gin_y, gin_c,
     ag_send, ag_recv, agp_send, agp_recv,
     fz_send, fz_recv, fx_send, fx_recv, bx_send, bx_recv,
-    p_send, p_recv, rr_send, rr_recv, rl_send, rl_recv, gs_send, gs_recv,
+    p_send, p_recv, rn_send, rn_recv, rf_send, rf_recv, gs_send, gs_recv,
 ):
     chan = lax.axis_index("chan")
     ctx = lax.axis_index("ctx")
     rep = lax.axis_index("rep")
     core, zl = lax.rem(chan, 2), lax.div(chan, 2)
     zh, xx = lax.rem(ctx, 2), lax.div(ctx, 2)
-    has_left, has_right = zl > 0, zl < 3
-    left, right, partner = {"chan": chan - 2}, {"chan": chan + 2}, {"chan": chan + 1 - 2 * core}
+    near_at, far_at = zl + 1 - 2 * lax.rem(zl, 2), zl + 2 - 4 * lax.div(zl, 2)
+    cross_at = near_at + 2 - 4 * lax.div(zl, 2)
+    near, far = {"chan": 2 * near_at + core}, {"chan": 2 * far_at + core}
+    partner = {"chan": chan + 1 - 2 * core}
     zpeer = {"ctx": ctx + 1 - 2 * zh}
     xpeer = [{"ctx": lax.rem(xx + i, 4) * 2 + zh} for i in (1, 2, 3)]
     cpeer = [{"ctx": lax.rem(ctx + i, 8)} for i in range(1, 8)]
@@ -70,16 +72,8 @@
     own_copy = pltpu.make_async_copy(d_ref, g_own.at[zl], own_sem)
     own_copy.start()
     barrier = pltpu.get_barrier_semaphore()
-    for dev in [partner] + cpeer + ypeer:
+    for dev in [partner, near, far] + cpeer + ypeer:
         pl.semaphore_signal(barrier, inc=1, device_id=dev, device_id_type=MESH)
-
-    @pl.when(has_left)
-    def _():
-        pl.semaphore_signal(barrier, inc=1, device_id=left, device_id_type=MESH)
-
-    @pl.when(has_right)
-    def _():
-        pl.semaphore_signal(barrier, inc=1, device_id=right, device_id_type=MESH)
 
     sel_row = jnp.where(lax.div(iota((32, 512), 1), 16) == iota((32, 512), 0), 1.0, 0.0).astype(F32)
     own_row = lax.rem(iota((16, 512), 1), 16) == iota((16, 512), 0)
@@ -107,74 +101,51 @@
         e_s[1, rows, :] = low
         e_p[rows, :] = (decay * left_over).astype(BF16)
 
-    pl.semaphore_wait(barrier, 11 + jnp.where(has_left, 1, 0) + jnp.where(has_right, 1, 0))
+    pl.semaphore_wait(barrier, 13)
 
     def half(h):
         return pl.ds(h * 128, 128)
 
-    def ag_right(src_ref, src, m, h):
-        return remote(
-            src_ref.at[half(h)], g_own.at[src, half(h)], ag_send.at[0, m, h], ag_recv.at[src, h], right
-        )
-
-    def ag_left(src_ref, src, m, h):
-        return remote(
-            src_ref.at[half(h)], g_own.at[src, half(h)], ag_send.at[1, m, h], ag_recv.at[src, h], left
-        )
+    def to_far(h):
+        return remote(d_ref.at[half(h)], g_own.at[zl, half(h)], ag_send.at[0, h], ag_recv.at[zl, h], far)
+
+    def to_near(h):
+        return remote(d_ref.at[half(h)], g_own.at[zl, half(h)], ag_send.at[1, h], ag_recv.at[zl, h], near)
+
+    def pass_on(h):
+        block = g_own.at[far_at, half(h)]
+        return remote(block, block, ag_send.at[2, h], ag_recv.at[far_at, h], near)
 
     def ag_partner(src_ref, src, h):
         return remote(
             src_ref.at[half(h)], g_par.at[src, half(h)], agp_send.at[src, h], agp_recv.at[src, h], partner
         )
 
+    def arrived(src, h):
+        block = g_own.at[src, half(h)]
+        remote(block, block, ag_send.at[2, h], ag_recv.at[src, h], near).wait_recv()
+
     for h in range(2):
-        @pl.when(has_right)
-        def _():
-            ag_right(d_ref, zl, 0, h).start()
-
-        @pl.when(has_left)
-        def _():
-            ag_left(d_ref, zl, 0, h).start()
-
+        to_far(h).start()
+    for h in range(2):
+        to_near(h).start()
     for h in range(2):
         ag_partner(d_ref, zl, h).start()
 
-    def ag_step(m, h):
-        src_l, src_r = zl - m, zl + m
-
-        @pl.when(src_l >= 0)
-        def _():
-            ag_right(g_own.at[src_l], src_l, 0, h).wait_recv()
-
-            if m < 3:
-                @pl.when(has_right)
-                def _():
-                    ag_right(g_own.at[src_l], src_l, m, h).start()
-
-            ag_partner(g_own.at[src_l], src_l, h).start()
-
-        @pl.when(src_r <= 3)
-        def _():
-            ag_left(g_own.at[src_r], src_r, 0, h).wait_recv()
-
-            if m < 3:
-                @pl.when(has_left)
-                def _():
-                    ag_left(g_own.at[src_r], src_r, m, h).start()
-
-            ag_partner(g_own.at[src_r], src_r, h).start()
+    def ag_far(h):
+        arrived(far_at, h)
+        pass_on(h).start()
+        ag_partner(g_own.at[far_at], far_at, h).start()
+
+    def ag_take(src, h):
+        arrived(src, h)
+        ag_partner(g_own.at[src], src, h).start()
 
     def ag_drain():
         for h in range(2):
-            for m in range(3):
-                @pl.when(jnp.logical_and(has_right, zl - m >= 0))
-                def _():
-                    ag_right(d_ref, zl, m, h).wait_send()
-
-                @pl.when(jnp.logical_and(has_left, zl + m <= 3))
-                def _():
-                    ag_left(d_ref, zl, m, h).wait_send()
-
+            to_far(h).wait_send()
+            to_near(h).wait_send()
+            pass_on(h).wait_send()
             for j in range(4):
                 ag_partner(d_ref, j, h).wait_send()
 
@@ -263,10 +234,10 @@
         fx.append(remote(pair_p, xin_p.at[i], fx_send.at[1, i], fx_recv.at[1, i], xpeer[i]))
         fx[-1].start()
 
-    ag_step(1, 0)
     conv_tile(1, 0, 4)
-    ag_step(1, 1)
+    ag_far(0)
     conv_tile(1, 4, 8)
+    ag_far(1)
 
     @pl.loop(0, 4)
     def _(i):
@@ -289,7 +260,6 @@
         e_q[1, rows, :] = low
         e_q1[rows, :] = (decay * lane256).astype(BF16)
 
-    ag_step(2, 0)
     for c in fx:
         c.wait_recv()
     sum_s = jnp.where(first, 0.0, zin_s[...])
@@ -338,43 +308,23 @@
         to_partner(j).wait_recv()
         pacc[j] += xbuf[j].astype(F32)
 
-    def rs_right(j, h):
-        return remote(snd_r.at[j, half(h)], rec_l.at[j, half(h)], rr_send.at[j, h], rr_recv.at[j, h], right)
-
-    def rs_left(j, h):
-        return remote(snd_l.at[j, half(h)], rec_r.at[j, half(h)], rl_send.at[j, h], rl_recv.at[j, h], left)
-
-    def rs_first(m, h):
-        jr, jl = 3 - m, m
-
-        @pl.when(zl == 0)
-        def _():
-            snd_r[jr, half(h)] = pacc[jr, half(h)].astype(BF16)
-            rs_right(jr, h).start()
-
-        @pl.when(zl == 3)
-        def _():
-            snd_l[jl, half(h)] = pacc[jl, half(h)].astype(BF16)
-            rs_left(jl, h).start()
-
-    def rs_hop(m, h):
-        jr, jl = 3 - m, m
-
-        @pl.when(jnp.logical_and(jr > zl, zl > 0))
-        def _():
-            rs_right(jr, h).wait_recv()
-            snd_r[jr, half(h)] = (pacc[jr, half(h)] + rec_l[jr, half(h)].astype(F32)).astype(BF16)
-            rs_right(jr, h).start()
-
-        @pl.when(jnp.logical_and(jl < zl, zl < 3))
-        def _():
-            rs_left(jl, h).wait_recv()
-            snd_l[jl, half(h)] = (pacc[jl, half(h)] + rec_r[jl, half(h)].astype(F32)).astype(BF16)
-            rs_left(jl, h).start()
-
-    for m in range(3):
+    def rs_near(k, h):
+        return remote(
+            snd_n.at[k, half(h)], rec_n.at[k, half(h)], rn_send.at[k, h], rn_recv.at[k, h], near
+        )
+
+    def rs_far(h):
+        return remote(snd_f.at[half(h)], rec_f.at[half(h)], rf_send.at[h], rf_recv.at[h], far)
+
+    for k, j in ((0, cross_at), (1, near_at)):
+        snd_n[k] = pacc[j].astype(BF16)
         for h in range(2):
-            rs_first(m, h)
+            rs_near(k, h).start()
+
+    def rs_service(h):
+        rs_near(0, h).wait_recv()
+        snd_f[half(h)] = (pacc[far_at, half(h)] + rec_n[0, half(h)].astype(F32)).astype(BF16)
+        rs_far(h).start()
 
     def back_own(j):
         back_ref[...] += dot(g_own[j], w_block(j, core))
@@ -384,31 +334,20 @@
             ag_partner(d_ref, j, h).wait_recv()
         back_ref[...] += dot(g_par[j], w_block(j, 1 - core))
 
-    def both_sides(act, m):
-        @pl.when(zl - m >= 0)
-        def _():
-            act(zl - m)
-
-        @pl.when(zl + m <= 3)
-        def _():
-            act(zl + m)
-
-    ag_step(2, 1)
     back_ref[...] = dot(g_own[zl], w_block(zl, core))
     back_par(zl)
+    for h in range(2):
+        ag_take(near_at, h)
+    back_own(far_at)
+    back_own(near_at)
+    back_par(far_at)
     taps_tile(0)
-    rs_hop(0, 0)
-    both_sides(back_own, 1)
-    both_sides(back_par, 1)
-    ag_step(3, 0)
-    rs_hop(0, 1)
+    back_par(near_at)
+    ag_take(cross_at, 0)
     taps_tile(1)
-    both_sides(back_own, 2)
-    both_sides(back_par, 2)
-    ag_step(3, 1)
-    both_sides(back_own, 3)
-    rs_hop(1, 0)
-    both_sides(back_par, 3)
+    ag_take(cross_at, 1)
+    back_own(cross_at)
+    back_par(cross_at)
 
     dconv_ref[...] = (q_ref[...].astype(F32) * back_ref[...]).astype(BF16)
     for tile in range(2):
@@ -417,7 +356,8 @@
         state_q[:, part] = fold(dot(e_q[0, part, :], dt) + dot(e_q[1, part, :], dt))
     bz = remote(state_q, zin_q, fz_send.at[2], fz_recv.at[2], zpeer)
     bz.start()
-    rs_hop(1, 1)
+    rs_service(0)
+    rs_service(1)
     for tile in range(2):
         part = slice(tile * 256, tile * 256 + 256)
         state_q1[:, part] = fold(dot(e_q1[part, :], dconv_ref[:, part]))
@@ -450,30 +390,7 @@
                 )
 
     mixed_tile(0)
-    rs_hop(2, 0)
     mixed_tile(1)
-    rs_hop(2, 1)
-
-    pick_pole = jnp.where(own_row, 1.0, 0.0).astype(F32)
-    pick_group = lax.div(iota((512, 32), 0), 16) == iota((512, 32), 1)
-
-    def param_sum(prod, cross):
-        column = jnp.sum(prod[...], axis=1, keepdims=True)
-        return dot_exact(pick_pole, jnp.where(pick_group, column, 0.0)) + dot_exact(cross, sel_row, 1, 1)
-
-    gsum[0] = jnp.zeros((32, 128), F32)
-    gsum[0, 0:16, 0:32] = param_sum(prod_res, state_q[...] * in_s[...])
-    gsum[0, 16:32, 0:32] = param_sum(prod_rate, state_q1[...] * in_s[...] + state_q[...] * in_p[...])
-
-    def exchange(src, dst, at, peers):
-        copies = []
-        for i, dev in enumerate(peers):
-            copies.append(remote(src, dst.at[i], gs_send.at[at + i], gs_recv.at[at + i], dev))
-            copies[-1].start()
-        return copies
-
-    started = exchange(gsum.at[0], gin_y, 0, ypeer)
-    dz_tile(0)
 
     bz.wait_recv()
     q_one = jnp.where(first, state_q[...], zin_q[...])
@@ -483,6 +400,27 @@
     for i in range(3):
         bx.append(remote(pair_q, xin_q.at[i], bx_send.at[i], bx_recv.at[i], xpeer[i]))
         bx[-1].start()
+
+    pick_pole = jnp.where(own_row, 1.0, 0.0).astype(F32)
+    pick_group = lax.div(iota((512, 32), 0), 16) == iota((512, 32), 1)
+
+    def param_sum(prod, cross):
+        column = jnp.sum(prod[...], axis=1, keepdims=True)
+        return dot_exact(pick_pole, jnp.where(pick_group, column, 0.0)) + dot_exact(cross, sel_row, 1, 1)
+
+    gsum[0] = jnp.zeros((32, 128), F32)
+    gsum[0, 0:16, 0:32] = param_sum(prod_res, state_q[...] * in_s[...])
+    gsum[0, 16:32, 0:32] = param_sum(prod_rate, state_q1[...] * in_s[...] + state_q[...] * in_p[...])
+
+    def exchange(src, dst, at, peers):
+        copies = []
+        for i, dev in enumerate(peers):
+            copies.append(remote(src, dst.at[i], gs_send.at[at + i], gs_recv.at[at + i], dev))
+            copies[-1].start()
+        return copies
+
+    started = exchange(gsum.at[0], gin_y, 0, ypeer)
+    dz_tile(0)
 
     for c in started:
         c.wait_recv()
@@ -507,6 +445,11 @@
         gv_ref[:, part] = (dz * k_ref[:, part].astype(F32)).astype(BF16)
         gk_ref[:, part] = (dz * v_ref[:, part].astype(F32)).astype(BF16)
 
+    for h in range(2):
+        rs_near(1, h).wait_recv()
+        rs_far(h).wait_recv()
+    out_ref[...] = (pacc[zl] + rec_n[1].astype(F32) + rec_f[...].astype(F32)).astype(BF16)
+
     for c in last:
         c.wait_recv()
     total = gsum[1]
@@ -515,32 +458,15 @@
     gres_ref[...] = total[0:16, 0:32]
     grate_ref[...] = -res_ref[...] * total[16:32, 0:32]
 
-    for h in range(2):
-        @pl.when(has_left)
-        def _():
-            rs_right(zl, h).wait_recv()
-            pacc[zl, half(h)] += rec_l[zl, half(h)].astype(F32)
-
-        @pl.when(has_right)
-        def _():
-            rs_left(zl, h).wait_recv()
-            pacc[zl, half(h)] += rec_r[zl, half(h)].astype(F32)
-
-    out_ref[...] = pacc[zl].astype(BF16)
-
     for c in fz + fx + bx + [bz] + started + last:
         c.wait_send()
     ag_drain()
     for j in range(4):
         to_partner(j).wait_send()
-        for h in range(2):
-            @pl.when(j > zl)
-            def _():
-                rs_right(j, h).wait_send()
-
-            @pl.when(j < zl)
-            def _():
-                rs_left(j, h).wait_send()
+    for h in range(2):
+        rs_near(0, h).wait_send()
+        rs_near(1, h).wait_send()
+        rs_far(h).wait_send()
 
 
 def hand_over(*refs):
@@ -569,11 +495,12 @@
         vm((256, 512), F32), vm((256, 512), F32),
         state(), state(), state(), state(), state(), state(), states(), states(), state(), state(),
         state(), state(), state(), state(), states(), state(),
-        blocks(), blocks(), vm((4, 256, 512), F32), blocks(), blocks(), blocks(), blocks(), blocks(), blocks(),
+        blocks(), blocks(), vm((4, 256, 512), F32), blocks(), blocks(),
+        vm((2, 256, 512), BF16), vm((2, 256, 512), BF16), vm((256, 512), BF16), vm((256, 512), BF16),
         vm((2, 32, 128), F32), vm((3, 32, 128), F32), vm((7, 32, 128), F32),
-        dma((2, 3, 2)), dma((4, 2)), dma((4, 2)), dma((4, 2)),
+        dma((3, 2)), dma((4, 2)), dma((4, 2)), dma((4, 2)),
         dma((3,)), dma((3,)), dma((2, 3)), dma((2, 3)), dma((3,)), dma((3,)),
-        dma((4,)), dma((4,)), dma((4, 2)), dma((4, 2)), dma((4, 2)), dma((4, 2)), dma((10,)), dma((10,)),
+        dma((4,)), dma((4,)), dma((2, 2)), dma((2, 2)), dma((2,)), dma((2,)), dma((10,)), dma((10,)),
     ]
     shapes = (act, act, act, act, par, par)
     results = pl.pallas_call(

time: 80.2 us -> 70.8 us (0.88)
  Pallas kernels: 79.5 us -> 70.1 us
    pallas_call x1, Pallas kernels: 77.3 us -> 67.9 us  [per_device(): pl.pallas_call(kernel, out_shape=shapes, in_specs=[spec, spec, spec, spec...]
where the time goes in v3:
time: 70.8 us; the launch traced here: 70.7 us
  Pallas kernels  70.1 us (99%)
    pallas_call x1, Pallas kernels, per_device(): pl.pallas_call(kernel, out_shape=shapes, in_specs=[spec, spec, spec, spec...  67.9 us
    pallas_call x1, Pallas kernels, per_device(): pl.pallas_call(hand_over, out_shape=shapes, in_specs=[spec] * 6, out_spec...  2.18 us

profile of v3, /device:TPU:32, one launch (start us, length us, event | category | flops | bytes accessed | tf_op | source)
XLA Modules:
  0.0 70.7 jit_solution(12543422985240640749)
XLA Ops:
  0.6 67.9 %hyena.1 = (bf16[256,512]{1,0:T(8,128)(2,1)}, bf16[256,512]{1,0:T(8,128)(2,1)}, bf16[256,512]{1,0:T(8,128)(2,1)}, bf16[256,512]{1,0:T(8,128)(2,1)}, f32[16,32]{1,0:T(8,128)}, /*index=5*/f32[16,32]{1,0:T(8,128)}) custom-call(bf16[256,512]{1,0:T(8,128)(2,1)} %bitcast.8, bf16[256,512]{1,0:T(8,128)(2,1)} %bitcast.9, bf16[256,512]{1,0:T(8,128)(2,1)} %bitcast.10, ...), custom_call_target="tpu_custom_call" | custom-call | tf_op jit(solution)/shard_map/hyena/pallas_call | solution.py:506
  68.5 2.2 %results.1 = (bf16[256,512]{1,0:T(8,128)(2,1)}, bf16[256,512]{1,0:T(8,128)(2,1)}, bf16[256,512]{1,0:T(8,128)(2,1)}, bf16[256,512]{1,0:T(8,128)(2,1)}, f32[16,32]{1,0:T(8,128)}, /*index=5*/f32[16,32]{1,0:T(8,128)}) custom-call(bf16[256,512]{1,0:T(8,128)(2,1)} %get-tuple-element.18.refs_0_, bf16[256,512]{1,0:T(8,128)(2,1)} %get-tuple-element.19.refs_1_, ...), custom_call_target="tpu_custom_call" | custom-call | tf_op jit(solution)/shard_map/results/pallas_call | solution.py:517
